TPU v7x, 32 devices: a whole 2x2x4 slice. The times are simulated.
32 devices in a mesh: team: 2 (over x), blk: 4 (over z), head: 4 (over y, core).
Axes of the slice: x: 2, y: 2, z: 4, core: 2. Of those that a mesh axis runs over, the one named last changes fastest.
Arguments:
- queries: bfloat16 [1024, 8, 8, 128], P('blk', 'head', 'team'), may hold values from -40 to 40
- features: bfloat16 [1024, 8192], P('blk', ('team', 'head')), may hold values from -6 to 6
- adapter_down: bfloat16 [4, 8192, 64], P(None, ('team', 'head')), may hold values from -0.0625 to 0.0625
- adapter_key_up: bfloat16 [4, 64, 8, 128], P(None, None, 'head'), may hold values from -0.75 to 0.75
- adapter_value_up: bfloat16 [4, 64, 8, 128], P(None, None, 'head'), may hold values from -0.75 to 0.75
- base_key: bfloat16 [1024, 8, 128], P('blk', 'head'), may hold values from -6 to 6
- base_value: bfloat16 [1024, 8, 128], P('blk', 'head'), may hold values from -24 to 24
- prefix_key: bfloat16 [2048, 8, 128], P('blk', 'head'), may hold values from -7 to 7
- prefix_value: bfloat16 [2048, 8, 128], P('blk', 'head'), may hold values from -24 to 24
- adapter_ids: int32 [4], replicated, may hold values from 0 to 3
- block_order: int32 [4], replicated, may hold values from 0 to 15
Outputs:
- attended: bfloat16 [1024, 8, 8, 128], P('blk', 'head', 'team')
All inputs are finite; a program needn't handle non-finite values.
Results may differ from a plain program's by a relative error of at most 0.011.
Values may be sent and summed in bfloat16 or wider, within the bound.
No kernel may reach another device: no remote copies, remote signals or barrier semaphores. Data moves between devices by JAX's collectives and lax.ppermute only.
A program may use at most 64 MiB of HBM per device.

v0:
```python
import math
import jax
import jax.numpy as jnp
from jax import lax
from jax.sharding import PartitionSpec as P

NEG_FILL = -1e30


def block_length(row_count):
    for candidate in range(min(row_count, 1024), 0, -1):
        if row_count % candidate == 0:
            return candidate
    return row_count


def key_positions(row_count, shard_rows, prefix_dev, query_dev, block_order, block_count):
    row_index = jnp.arange(row_count, dtype=jnp.int32)
    holder = row_index // shard_rows
    within = row_index - holder * shard_rows
    block_ids = jnp.arange(block_count, dtype=jnp.int32)
    holder_order = jnp.sum(
        jnp.where(holder[:, None] == block_ids[None, :], block_order[None, :], 0), axis=1
    )
    later = prefix_dev * block_count + holder_order * query_dev + within - prefix_dev
    return jnp.where(within < prefix_dev, holder * prefix_dev + within, later)


def attend(running, query_rows, query_pos, key_rows, value_rows, key_pos):
    row_count = key_rows.shape[0]
    block_rows = block_length(row_count)
    key_blocks = row_count // block_rows
    kv_heads = key_rows.shape[1]
    head_dim = key_rows.shape[2]
    score_scale = 1.0 / math.sqrt(head_dim)
    latest = jnp.max(query_pos)
    key_split = key_rows.reshape((key_blocks, block_rows, kv_heads, head_dim))
    value_split = value_rows.reshape((key_blocks, block_rows, kv_heads, head_dim))
    pos_split = key_pos.reshape((key_blocks, block_rows))

    def advance(carried, block_data):
        block_keys, block_values, block_pos = block_data

        def compute(previous):
            row_max, row_sum, weighted = previous
            scores = (
                jnp.einsum(
                    "tkgd,skd->kgts", query_rows, block_keys, preferred_element_type=jnp.float32
                )
                * score_scale
            )
            visible = block_pos[None, None, None, :] <= query_pos[None, None, :, None]
            scores = jnp.where(visible, scores, NEG_FILL)
            new_max = jnp.maximum(row_max, jnp.max(scores, axis=-1))
            weights = jnp.where(visible, jnp.exp(scores - new_max[..., None]), 0.0)
            factor = jnp.exp(row_max - new_max)
            row_sum = row_sum * factor + jnp.sum(weights, axis=-1)
            product = jnp.einsum(
                "kgts,skd->kgtd",
                weights.astype(jnp.bfloat16),
                block_values,
                preferred_element_type=jnp.float32,
            )
            weighted = weighted * factor[..., None] + product
            return (new_max, row_sum, weighted)

        return (lax.cond(jnp.min(block_pos) > latest, lambda kept: kept, compute, carried), None)

    result, _ = lax.scan(advance, running, (key_split, value_split, pos_split))
    return result


def on_device(
    queries,
    features,
    adapter_down,
    adapter_key_up,
    adapter_value_up,
    base_key,
    base_value,
    prefix_key,
    prefix_value,
    adapter_ids,
    block_order,
):
    block_count = lax.axis_size("blk")
    my_block = lax.axis_index("blk")
    query_dev = queries.shape[0]
    kv_heads = queries.shape[1]
    group_dev = queries.shape[2]
    head_dim = queries.shape[3]
    prefix_dev = prefix_key.shape[0]
    rank_width = adapter_down.shape[2]
    shard_rows = prefix_dev + query_dev
    chosen = adapter_ids[my_block]
    down_rows = lax.dynamic_index_in_dim(adapter_down, chosen, 0, keepdims=False)
    partial_latent = jnp.dot(features, down_rows, preferred_element_type=jnp.float32)
    latent = lax.psum(partial_latent, ("team", "head")).astype(jnp.bfloat16)

    def expand(up_table, base_rows):
        up_rows = lax.dynamic_index_in_dim(up_table, chosen, 0, keepdims=False).reshape(
            rank_width, kv_heads * head_dim
        )
        delta = jnp.dot(latent, up_rows, preferred_element_type=jnp.float32).reshape(
            query_dev, kv_heads, head_dim
        )
        return (base_rows.astype(jnp.float32) + delta).astype(jnp.bfloat16)

    key_rows = jnp.concatenate([prefix_key, expand(adapter_key_up, base_key)], axis=0)
    value_rows = jnp.concatenate([prefix_value, expand(adapter_value_up, base_value)], axis=0)
    prefix_total = prefix_dev * block_count
    offsets = jnp.arange(query_dev, dtype=jnp.int32)
    query_pos = prefix_total + block_order[my_block] * query_dev + offsets
    initial = (
        jnp.full((kv_heads, group_dev, query_dev), NEG_FILL, jnp.float32),
        jnp.zeros((kv_heads, group_dev, query_dev), jnp.float32),
        jnp.zeros((kv_heads, group_dev, query_dev, head_dim), jnp.float32),
    )
    key_piece = lax.all_gather(key_rows, "blk", axis=0, tiled=True)
    value_piece = lax.all_gather(value_rows, "blk", axis=0, tiled=True)
    piece_pos = key_positions(
        key_piece.shape[0], shard_rows, prefix_dev, query_dev, block_order, block_count
    )
    row_max, row_sum, weighted = attend(
        initial, queries, query_pos, key_piece, value_piece, piece_pos
    )
    result = weighted / row_sum[..., None]
    return result.transpose(2, 0, 1, 3).astype(jnp.bfloat16)


def solution(mesh):
    placed = (
        P("blk", "head", "team", None),
        P("blk", ("team", "head")),
        P(None, ("team", "head"), None),
        P(None, None, "head", None),
        P(None, None, "head", None),
        P("blk", "head", None),
        P("blk", "head", None),
        P("blk", "head", None),
        P("blk", "head", None),
        P(),
        P(),
    )
    return jax.shard_map(
        on_device,
        mesh=mesh,
        in_specs=placed,
        out_specs=P("blk", "head", "team", None),
        check_vma=False,
    )
```

profile of v0, /device:TPU:0, one launch (start us, length us, event | category | flops | bytes accessed | tf_op | source)
XLA Modules:
  0.0 160.4 jit_solution(10820601032562232662)
XLA Ops:
  6.5 1.3 dynamic_slice.39
  9.8 1.2 convolution_bitcast_fusion
  11.0 26.0 %psum.7 = bf16[256,64]{0,1:T(8,128)(2,1)S(1)} all-reduce(f32[256,64]{0,1:T(8,128)S(1)} %convolution_bitcast_fusion), channel_id=1, replica_groups=mesh['team'=2,'blk'=4,'head'=4] {'team','head'}, use_global_device_ids=true, to_apply=%region_0.1 | all-reduce | flops 16384 | bytes 98304 | tf_op jit(solution)/shard_map/psum | solution.py:98
  41.8 1.1 fusion.22
  43.7 1.2 dynamic_slice.38
  46.1 1.1 copy.40
  48.1 29.3 %all-gather.3.cloned.1.call-done = bf16[3072,2,128]{2,0,1:T(8,128)(2,1)} async-done(((bf16[768,2,128]{2,0,1:T(8,128)(2,1)}), bf16[3072,2,128]{2,0,1:T(8,128)(2,1)}) %all-gather.3.cloned.1.call-update) | async-done | bytes 1572880 | tf_op jit(solution)/shard_map/all_gather | solution.py:119
  77.4 1.5 copy.39
  78.9 36.0 %all-gather.5.cloned.1.call-done = bf16[3072,2,128]{2,0,1:T(8,128)(2,1)} async-done(((bf16[768,2,128]{2,0,1:T(8,128)(2,1)}), bf16[3072,2,128]{2,0,1:T(8,128)(2,1)}) %all-gather.5.cloned.1.call-update) | async-done | bytes 1572880 | tf_op jit(solution)/shard_map/all_gather | solution.py:120
  114.9 2.7 %copy.41 = bf16[3,1024,2,128]{3,1,2,0:T(8,128)(2,1)} copy(bf16[3,1024,2,128]{3,1,0,2:T(8,128)(2,1)} %bitcast.83) | data formatting | bytes 3145728
  118.6 31.8 %while.15 = (s32[]{:T(128)}, f32[2,4,256]{2,1,0:T(4,128)S(1)}, f32[2,4,256]{2,1,0:T(4,128)S(1)}, f32[2,4,256,128]{3,2,1,0:T(8,128)}, s32[3,1024]{1,0:T(4,128)S(1...) while((s32[]{:T(128)}, f32[2,4,256]{2,1,0:T(4,128)S(1)}, ...), condition=%wide.region_9.10_spmd.clone, body=%wide.region_3.9_spmd.clone.sunk | while | flops 1101796608 | bytes 38421312 | solution.py:69
  120.5 8.7 %conditional.3 = (f32[2,4,256]{2,1,0:T(4,128)S(1)}, f32[2,4,256]{2,1,0:T(4,128)S(1)}, f32[2,4,256,128]{3,2,1,0:T(8,128)}) conditional(s32[]{:T(128)} %convert_element_type.57, (s32[1,1024]{1,0:T(1,128)S(1)}, s32[]{:T(128)}, bf16[3,1024,2,128]{3,1,2,0:T(8,128)(2,1)S(1)}, s32[]{:T(128)}, bf16[256,2,4,128]{3,0,2,1:T(8,128)(2,1)S(1)}, ...), branch_computations={%region_5.7_spmd, %region_8.8_spmd} | conditional | flops 1101795584 | bytes 38395480 | solution.py:67
  120.7 1.4 fusion.2
  122.2 2.0 %fusion.4 = f32[2,4,256]{2,1,0:T(4,128)S(1)} fusion(f32[2,1024,256,4]{2,1,3,0:T(8,128)S(1)} %get-tuple-element.228, f32[2,4,256]{2,1,0:T(4,128)S(1)} %max.4, pred[256,1024]{0,1:T(8,128)(4,1)S(1)} %broadcast_compare_fusion), kind=kLoop, calls=%fused_computation.5 | loop fusion | flops 10483712 | bytes 8667136 | tf_op jit(solution)/shard_map/while/body/eval_jaxpr/cond/branch_0_fun/reduce_sum | solution.py:57
  124.2 4.0 %fusion.8 = f32[2,4,256,128]{3,2,1,0:T(8,128)S(1)} fusion(f32[2,1024,256,4]{2,1,3,0:T(8,128)S(1)} %get-tuple-element.228, f32[2,4,256]{2,1,0:T(4,128)S(1)} %max.4, pred[256,1024]{0,1:T(8,128)(4,1)S(1)} %broadcast_compare_fusion, f32[2,4,256,128]{3,2,1,0:T(8,128)S(1)} %copy-done.1, bf16[3,1024,2,128]{3,1,2,0:T(8,128)(2,1)} %get-tuple-element.125, ...), kind=kOutput, calls=%fused_computation.8 | convolution fusion | flops 547880960 | bytes 11289088 | tf_op jit(solution)/shard_map/while/body/eval_jaxpr/cond/branch_0_fun/kgts,skd->kgtd/dot_general | solution.py:58
  131.1 8.7 %conditional.3 = (f32[2,4,256]{2,1,0:T(4,128)S(1)}, f32[2,4,256]{2,1,0:T(4,128)S(1)}, f32[2,4,256,128]{3,2,1,0:T(8,128)}) conditional(s32[]{:T(128)} %convert_element_type.57, (s32[1,1024]{1,0:T(1,128)S(1)}, s32[]{:T(128)}, bf16[3,1024,2,128]{3,1,2,0:T(8,128)(2,1)S(1)}, s32[]{:T(128)}, bf16[256,2,4,128]{3,0,2,1:T(8,128)(2,1)S(1)}, ...), branch_computations={%region_5.7_spmd, %region_8.8_spmd} | conditional | flops 1101795584 | bytes 38395480 | solution.py:67
  131.3 1.4 fusion.2
  132.8 2.0 %fusion.4 = f32[2,4,256]{2,1,0:T(4,128)S(1)} fusion(f32[2,1024,256,4]{2,1,3,0:T(8,128)S(1)} %get-tuple-element.228, f32[2,4,256]{2,1,0:T(4,128)S(1)} %max.4, pred[256,1024]{0,1:T(8,128)(4,1)S(1)} %broadcast_compare_fusion), kind=kLoop, calls=%fused_computation.5 | loop fusion | flops 10483712 | bytes 8667136 | tf_op jit(solution)/shard_map/while/body/eval_jaxpr/cond/branch_0_fun/reduce_sum | solution.py:57
  134.8 4.0 %fusion.8 = f32[2,4,256,128]{3,2,1,0:T(8,128)S(1)} fusion(f32[2,1024,256,4]{2,1,3,0:T(8,128)S(1)} %get-tuple-element.228, f32[2,4,256]{2,1,0:T(4,128)S(1)} %max.4, pred[256,1024]{0,1:T(8,128)(4,1)S(1)} %broadcast_compare_fusion, f32[2,4,256,128]{3,2,1,0:T(8,128)S(1)} %copy-done.1, bf16[3,1024,2,128]{3,1,2,0:T(8,128)(2,1)} %get-tuple-element.125, ...), kind=kOutput, calls=%fused_computation.8 | convolution fusion | flops 547880960 | bytes 11289088 | tf_op jit(solution)/shard_map/while/body/eval_jaxpr/cond/branch_0_fun/kgts,skd->kgtd/dot_general | solution.py:58
  141.7 8.7 %conditional.3 = (f32[2,4,256]{2,1,0:T(4,128)S(1)}, f32[2,4,256]{2,1,0:T(4,128)S(1)}, f32[2,4,256,128]{3,2,1,0:T(8,128)}) conditional(s32[]{:T(128)} %convert_element_type.57, (s32[1,1024]{1,0:T(1,128)S(1)}, s32[]{:T(128)}, bf16[3,1024,2,128]{3,1,2,0:T(8,128)(2,1)S(1)}, s32[]{:T(128)}, bf16[256,2,4,128]{3,0,2,1:T(8,128)(2,1)S(1)}, ...), branch_computations={%region_5.7_spmd, %region_8.8_spmd} | conditional | flops 1101795584 | bytes 38395480 | solution.py:67
  141.9 1.4 fusion.2
  143.4 2.0 %fusion.4 = f32[2,4,256]{2,1,0:T(4,128)S(1)} fusion(f32[2,1024,256,4]{2,1,3,0:T(8,128)S(1)} %get-tuple-element.228, f32[2,4,256]{2,1,0:T(4,128)S(1)} %max.4, pred[256,1024]{0,1:T(8,128)(4,1)S(1)} %broadcast_compare_fusion), kind=kLoop, calls=%fused_computation.5 | loop fusion | flops 10483712 | bytes 8667136 | tf_op jit(solution)/shard_map/while/body/eval_jaxpr/cond/branch_0_fun/reduce_sum | solution.py:57
  145.4 4.0 %fusion.8 = f32[2,4,256,128]{3,2,1,0:T(8,128)S(1)} fusion(f32[2,1024,256,4]{2,1,3,0:T(8,128)S(1)} %get-tuple-element.228, f32[2,4,256]{2,1,0:T(4,128)S(1)} %max.4, pred[256,1024]{0,1:T(8,128)(4,1)S(1)} %broadcast_compare_fusion, f32[2,4,256,128]{3,2,1,0:T(8,128)S(1)} %copy-done.1, bf16[3,1024,2,128]{3,1,2,0:T(8,128)(2,1)} %get-tuple-element.125, ...), kind=kOutput, calls=%fused_computation.8 | convolution fusion | flops 547880960 | bytes 11289088 | tf_op jit(solution)/shard_map/while/body/eval_jaxpr/cond/branch_0_fun/kgts,skd->kgtd/dot_general | solution.py:58
  150.6 2.9 %fusion.24 = bf16[256,2,4,128]{3,2,1,0:T(4,128)(2,1)} fusion(f32[2,4,256]{1,0,2:T(2,128)S(1)} %copy.42, f32[2,4,256,128]{3,2,1,0:T(8,128)} %get-tuple-element.142), kind=kLoop, calls=%fused_computation.31 | loop fusion | flops 524288 | bytes 1581056 | tf_op jit(solution)/shard_map/convert_element_type | solution.py:128
  (55 shorter events, 13.7 us)
Async XLA Ops:
  6.5 3.2 %copy-start = (bf16[256,1024]{1,0:T(8,128)(2,1)S(1)}, bf16[256,1024]{1,0:T(8,128)(2,1)}, u32[]{:S(2)}) copy-start(bf16[256,1024]{1,0:T(8,128)(2,1)} %param.16) | copy-start | bytes 1572868
  6.5 70.8 %all-gather.3.cloned.1.call-start = ((), (), s32[]{:S(2)}) async-start(), calls=%async_computation | async-start | bytes 1966080 | tf_op jit(solution)/shard_map/all_gather | solution.py:119
  40.7 74.2 %all-gather.5.cloned.1.call-start = ((), (), s32[]{:S(2)}) async-start(), calls=%async_computation.1 | async-start | bytes 1966080 | tf_op jit(solution)/shard_map/all_gather | solution.py:120
  120.7 3.5 %copy-start.1 = (f32[2,4,256,128]{3,2,1,0:T(8,128)S(1)}, f32[2,4,256,128]{3,2,1,0:T(8,128)}, u32[]{:S(2)}) copy-start(f32[2,4,256,128]{3,2,1,0:T(8,128)} %get-tuple-element.124) | copy-start | bytes 3145732 | tf_op jit(solution)/shard_map/while/body/eval_jaxpr/cond
  128.3 1.0 copy-start.2
  131.3 3.5 %copy-start.1 = (f32[2,4,256,128]{3,2,1,0:T(8,128)S(1)}, f32[2,4,256,128]{3,2,1,0:T(8,128)}, u32[]{:S(2)}) copy-start(f32[2,4,256,128]{3,2,1,0:T(8,128)} %get-tuple-element.124) | copy-start | bytes 3145732 | tf_op jit(solution)/shard_map/while/body/eval_jaxpr/cond
  138.9 1.0 copy-start.2
  141.9 3.5 %copy-start.1 = (f32[2,4,256,128]{3,2,1,0:T(8,128)S(1)}, f32[2,4,256,128]{3,2,1,0:T(8,128)}, u32[]{:S(2)}) copy-start(f32[2,4,256,128]{3,2,1,0:T(8,128)} %get-tuple-element.124) | copy-start | bytes 3145732 | tf_op jit(solution)/shard_map/while/body/eval_jaxpr/cond
  149.5 1.0 copy-start.2
Sparse Core Ops, SparseCore 0:
  40.8 36.4 all-gather.2
  78.9 35.9 all-gather.4
where the time goes:
time: 161 us; the launch traced here: 160 us
  waiting for transfers between devices  65.4 us (41%)
  blocking collectives  26 us (16%)
  matrix products  19.7 us (12%)
  between operations  16 us (10%)
  local copies, waits for them, and re-layouts  14.8 us (9%)
  other arithmetic  14.6 us (9%)
  loops' own time  3.9 us (2%)
    all_gather x1, waiting for transfers between devices, on_device(): value_piece = lax.all_gather(value_rows, 'blk', axis=0, tiled=True)  36 us
    all_gather x1, waiting for transfers between devices, on_device(): key_piece = lax.all_gather(key_rows, 'blk', axis=0, tiled=True)  29.3 us
    psum x1, blocking collectives, on_device(): latent = lax.psum(partial_latent, ('team', 'head')).astype(jnp.bfloat16)  26 us
    dot_general x3, matrix products, compute(): jnp.einsum('kgts,skd->kgtd', weights.astype(jnp.bfloat16), block_values,...  12.1 us
    unnamed x7, local copies, waits for them, and re-layouts  7.28 us
    reduce_sum x3, other arithmetic, compute(): row_sum = row_sum * factor + jnp.sum(weights, axis=-1)  6.09 us
    dot_general x3, matrix products, compute(): jnp.einsum('tkgd,skd->kgts', query_rows, block_keys, preferred_element_ty...  4.2 us
    another operation x1, loops' own time, attend(): result, _ = lax.scan(advance, running, (key_split, value_split, pos_split))  3.67 us
  transfers between devices with their start and end apart: 2, of which 2 were waited for; matrix products, arithmetic and copies ran while one was open for 5% of the time, Pallas kernels for 0%

commit v1 on v0

--- a/solution.py
+++ b/solution.py
@@ -95,7 +95,7 @@
     chosen = adapter_ids[my_block]
     down_rows = lax.dynamic_index_in_dim(adapter_down, chosen, 0, keepdims=False)
     partial_latent = jnp.dot(features, down_rows, preferred_element_type=jnp.float32)
-    latent = lax.psum(partial_latent, ("team", "head")).astype(jnp.bfloat16)
+    latent = lax.psum(lax.psum(partial_latent, "head"), "team").astype(jnp.bfloat16)
 
     def expand(up_table, base_rows):
         up_rows = lax.dynamic_index_in_dim(up_table, chosen, 0, keepdims=False).reshape(

time: 161 us -> 177 us (1.099)
  waiting for transfers between devices: 65.4 us -> 97.6 us
  blocking collectives: 26 us -> 9.44 us
    psum x0 -> x1, waiting for transfers between devices: none -> 32.5 us  [on_device(): lax.psum(partial_latent, 'head')]
    psum x1, blocking collectives: 26 us -> 9.44 us  [on_device(): lax.psum(lax.psum(partial_latent, 'head'), 'team').astype(jnp.bfloat16)]
  transfers between devices with their start and end apart: 2 -> 3, of which waited for: 2 -> 3; matrix products, arithmetic and copies ran while one was open for 5% -> 6% of each run, Pallas kernels for 0% -> 0%
where the time goes in v1:
time: 177 us; the launch traced here: 176 us
  waiting for transfers between devices  97.6 us (55%)
  matrix products  20.4 us (12%)
  between operations  15.7 us (9%)
  local copies, waits for them, and re-layouts  14.8 us (8%)
  other arithmetic  14.6 us (8%)
  blocking collectives  9.44 us (5%)
  loops' own time  3.9 us (2%)
    all_gather x1, waiting for transfers between devices, on_device(): value_piece = lax.all_gather(value_rows, 'blk', axis=0, tiled=True)  36 us
    psum x1, waiting for transfers between devices, on_device(): lax.psum(partial_latent, 'head')  32.5 us
    all_gather x1, waiting for transfers between devices, on_device(): key_piece = lax.all_gather(key_rows, 'blk', axis=0, tiled=True)  29 us
    dot_general x3, matrix products, compute(): jnp.einsum('kgts,skd->kgtd', weights.astype(jnp.bfloat16), block_values,...  12.1 us
    psum x1, blocking collectives, on_device(): lax.psum(lax.psum(partial_latent, 'head'), 'team').astype(jnp.bfloat16)  9.44 us
    unnamed x7, local copies, waits for them, and re-layouts  7.28 us
    reduce_sum x3, other arithmetic, compute(): row_sum = row_sum * factor + jnp.sum(weights, axis=-1)  6.09 us
    dot_general x3, matrix products, compute(): jnp.einsum('tkgd,skd->kgts', query_rows, block_keys, preferred_element_ty...  4.2 us
  transfers between devices with their start and end apart: 3, of which 3 were waited for; matrix products, arithmetic and copies ran while one was open for 6% of the time, Pallas kernels for 0%

profile of v1, /device:TPU:0, one launch (start us, length us, event | category | flops | bytes accessed | tf_op | source)
XLA Modules:
  0.0 176.5 jit_solution(5604403744250733096)
XLA Ops:
  6.5 1.3 dynamic_slice.39
  9.8 1.8 %convolution_bitcast_fusion = f32[256,64]{0,1:T(8,128)} fusion(bf16[256,1024]{1,0:T(8,128)(2,1)S(1)} %copy-done, bf16[4,1024,64]{1,2,0:T(8,128)(2,1)} %param.17, s32[]{:T(128)S(6)} %select_n.51), kind=kOutput, calls=%fused_computation.28 | convolution fusion | flops 33554432 | bytes 720900 | tf_op jit(solution)/shard_map/dot_general | solution.py:97
  13.5 32.5 %all-reduce.2.cloned.1.call-done = f32[256,64]{0,1:T(8,128)} async-done(((f32[256,64]{0,1:T(8,128)}), f32[256,64]{0,1:T(8,128)}) %all-reduce.2.cloned.1.call-update) | async-done | bytes 65552 | tf_op jit(solution)/shard_map/psum | solution.py:98
  46.0 9.4 %psum.15 = bf16[256,64]{0,1:T(8,128)(2,1)S(1)} all-reduce(f32[256,64]{0,1:T(8,128)} %all-reduce.2.cloned.1.call-done), channel_id=1, replica_groups=mesh['team'=2,'blk'=4,'head'=4] {'team'}, use_global_device_ids=true, to_apply=%region_1.2 | all-reduce | flops 16384 | bytes 98304 | tf_op jit(solution)/shard_map/psum | solution.py:98
  60.4 1.2 dynamic_slice.38
  62.8 1.1 copy.40
  64.8 29.0 %all-gather.3.cloned.1.call-done = bf16[3072,2,128]{2,0,1:T(8,128)(2,1)} async-done(((bf16[768,2,128]{2,0,1:T(8,128)(2,1)}), bf16[3072,2,128]{2,0,1:T(8,128)(2,1)}) %all-gather.3.cloned.1.call-update) | async-done | bytes 1572880 | tf_op jit(solution)/shard_map/all_gather | solution.py:119
  93.8 1.5 copy.39
  95.3 36.0 %all-gather.5.cloned.1.call-done = bf16[3072,2,128]{2,0,1:T(8,128)(2,1)} async-done(((bf16[768,2,128]{2,0,1:T(8,128)(2,1)}), bf16[3072,2,128]{2,0,1:T(8,128)(2,1)}) %all-gather.5.cloned.1.call-update) | async-done | bytes 1572880 | tf_op jit(solution)/shard_map/all_gather | solution.py:120
  131.3 2.7 %copy.41 = bf16[3,1024,2,128]{3,1,2,0:T(8,128)(2,1)} copy(bf16[3,1024,2,128]{3,1,0,2:T(8,128)(2,1)} %bitcast.83) | data formatting | bytes 3145728
  135.0 31.8 %while.15 = (s32[]{:T(128)}, f32[2,4,256]{2,1,0:T(4,128)S(1)}, f32[2,4,256]{2,1,0:T(4,128)S(1)}, f32[2,4,256,128]{3,2,1,0:T(8,128)}, s32[3,1024]{1,0:T(4,128)S(1...) while((s32[]{:T(128)}, f32[2,4,256]{2,1,0:T(4,128)S(1)}, ...), condition=%wide.region_10.11_spmd.clone, body=%wide.region_4.10_spmd.clone.sunk | while | flops 1101796608 | bytes 38421312 | solution.py:69
  136.9 8.7 %conditional.3 = (f32[2,4,256]{2,1,0:T(4,128)S(1)}, f32[2,4,256]{2,1,0:T(4,128)S(1)}, f32[2,4,256,128]{3,2,1,0:T(8,128)}) conditional(s32[]{:T(128)} %convert_element_type.57, (s32[1,1024]{1,0:T(1,128)S(1)}, s32[]{:T(128)}, bf16[3,1024,2,128]{3,1,2,0:T(8,128)(2,1)S(1)}, s32[]{:T(128)}, bf16[256,2,4,128]{3,0,2,1:T(8,128)(2,1)S(1)}, ...), branch_computations={%region_6.8_spmd, %region_9.9_spmd} | conditional | flops 1101795584 | bytes 38395480 | solution.py:67
  137.1 1.4 fusion.2
  138.5 2.0 %fusion.4 = f32[2,4,256]{2,1,0:T(4,128)S(1)} fusion(f32[2,1024,256,4]{2,1,3,0:T(8,128)S(1)} %get-tuple-element.228, f32[2,4,256]{2,1,0:T(4,128)S(1)} %max.4, pred[256,1024]{0,1:T(8,128)(4,1)S(1)} %broadcast_compare_fusion), kind=kLoop, calls=%fused_computation.5 | loop fusion | flops 10483712 | bytes 8667136 | tf_op jit(solution)/shard_map/while/body/eval_jaxpr/cond/branch_0_fun/reduce_sum | solution.py:57
  140.6 4.0 %fusion.8 = f32[2,4,256,128]{3,2,1,0:T(8,128)S(1)} fusion(f32[2,1024,256,4]{2,1,3,0:T(8,128)S(1)} %get-tuple-element.228, f32[2,4,256]{2,1,0:T(4,128)S(1)} %max.4, pred[256,1024]{0,1:T(8,128)(4,1)S(1)} %broadcast_compare_fusion, f32[2,4,256,128]{3,2,1,0:T(8,128)S(1)} %copy-done.1, bf16[3,1024,2,128]{3,1,2,0:T(8,128)(2,1)} %get-tuple-element.125, ...), kind=kOutput, calls=%fused_computation.8 | convolution fusion | flops 547880960 | bytes 11289088 | tf_op jit(solution)/shard_map/while/body/eval_jaxpr/cond/branch_0_fun/kgts,skd->kgtd/dot_general | solution.py:58
  147.5 8.7 %conditional.3 = (f32[2,4,256]{2,1,0:T(4,128)S(1)}, f32[2,4,256]{2,1,0:T(4,128)S(1)}, f32[2,4,256,128]{3,2,1,0:T(8,128)}) conditional(s32[]{:T(128)} %convert_element_type.57, (s32[1,1024]{1,0:T(1,128)S(1)}, s32[]{:T(128)}, bf16[3,1024,2,128]{3,1,2,0:T(8,128)(2,1)S(1)}, s32[]{:T(128)}, bf16[256,2,4,128]{3,0,2,1:T(8,128)(2,1)S(1)}, ...), branch_computations={%region_6.8_spmd, %region_9.9_spmd} | conditional | flops 1101795584 | bytes 38395480 | solution.py:67
  147.7 1.4 fusion.2
  149.1 2.0 %fusion.4 = f32[2,4,256]{2,1,0:T(4,128)S(1)} fusion(f32[2,1024,256,4]{2,1,3,0:T(8,128)S(1)} %get-tuple-element.228, f32[2,4,256]{2,1,0:T(4,128)S(1)} %max.4, pred[256,1024]{0,1:T(8,128)(4,1)S(1)} %broadcast_compare_fusion), kind=kLoop, calls=%fused_computation.5 | loop fusion | flops 10483712 | bytes 8667136 | tf_op jit(solution)/shard_map/while/body/eval_jaxpr/cond/branch_0_fun/reduce_sum | solution.py:57
  151.2 4.0 %fusion.8 = f32[2,4,256,128]{3,2,1,0:T(8,128)S(1)} fusion(f32[2,1024,256,4]{2,1,3,0:T(8,128)S(1)} %get-tuple-element.228, f32[2,4,256]{2,1,0:T(4,128)S(1)} %max.4, pred[256,1024]{0,1:T(8,128)(4,1)S(1)} %broadcast_compare_fusion, f32[2,4,256,128]{3,2,1,0:T(8,128)S(1)} %copy-done.1, bf16[3,1024,2,128]{3,1,2,0:T(8,128)(2,1)} %get-tuple-element.125, ...), kind=kOutput, calls=%fused_computation.8 | convolution fusion | flops 547880960 | bytes 11289088 | tf_op jit(solution)/shard_map/while/body/eval_jaxpr/cond/branch_0_fun/kgts,skd->kgtd/dot_general | solution.py:58
  158.1 8.7 %conditional.3 = (f32[2,4,256]{2,1,0:T(4,128)S(1)}, f32[2,4,256]{2,1,0:T(4,128)S(1)}, f32[2,4,256,128]{3,2,1,0:T(8,128)}) conditional(s32[]{:T(128)} %convert_element_type.57, (s32[1,1024]{1,0:T(1,128)S(1)}, s32[]{:T(128)}, bf16[3,1024,2,128]{3,1,2,0:T(8,128)(2,1)S(1)}, s32[]{:T(128)}, bf16[256,2,4,128]{3,0,2,1:T(8,128)(2,1)S(1)}, ...), branch_computations={%region_6.8_spmd, %region_9.9_spmd} | conditional | flops 1101795584 | bytes 38395480 | solution.py:67
  158.3 1.4 fusion.2
  159.7 2.0 %fusion.4 = f32[2,4,256]{2,1,0:T(4,128)S(1)} fusion(f32[2,1024,256,4]{2,1,3,0:T(8,128)S(1)} %get-tuple-element.228, f32[2,4,256]{2,1,0:T(4,128)S(1)} %max.4, pred[256,1024]{0,1:T(8,128)(4,1)S(1)} %broadcast_compare_fusion), kind=kLoop, calls=%fused_computation.5 | loop fusion | flops 10483712 | bytes 8667136 | tf_op jit(solution)/shard_map/while/body/eval_jaxpr/cond/branch_0_fun/reduce_sum | solution.py:57
  161.8 4.0 %fusion.8 = f32[2,4,256,128]{3,2,1,0:T(8,128)S(1)} fusion(f32[2,1024,256,4]{2,1,3,0:T(8,128)S(1)} %get-tuple-element.228, f32[2,4,256]{2,1,0:T(4,128)S(1)} %max.4, pred[256,1024]{0,1:T(8,128)(4,1)S(1)} %broadcast_compare_fusion, f32[2,4,256,128]{3,2,1,0:T(8,128)S(1)} %copy-done.1, bf16[3,1024,2,128]{3,1,2,0:T(8,128)(2,1)} %get-tuple-element.125, ...), kind=kOutput, calls=%fused_computation.8 | convolution fusion | flops 547880960 | bytes 11289088 | tf_op jit(solution)/shard_map/while/body/eval_jaxpr/cond/branch_0_fun/kgts,skd->kgtd/dot_general | solution.py:58
  167.0 2.9 %fusion.24 = bf16[256,2,4,128]{3,2,1,0:T(4,128)(2,1)} fusion(f32[2,4,256]{1,0,2:T(2,128)S(1)} %copy.42, f32[2,4,256,128]{3,2,1,0:T(8,128)} %get-tuple-element.142), kind=kLoop, calls=%fused_computation.31 | loop fusion | flops 524288 | bytes 1581056 | tf_op jit(solution)/shard_map/convert_element_type | solution.py:128
  (58 shorter events, 14.9 us)
Async XLA Ops:
  6.5 3.2 %copy-start = (bf16[256,1024]{1,0:T(8,128)(2,1)S(1)}, bf16[256,1024]{1,0:T(8,128)(2,1)}, u32[]{:S(2)}) copy-start(bf16[256,1024]{1,0:T(8,128)(2,1)} %param.16) | copy-start | bytes 1572868
  6.5 39.5 %all-reduce.2.cloned.1.call-start = ((), (), s32[]{:S(2)}) async-start(), calls=%async_computation | async-start | bytes 131072 | tf_op jit(solution)/shard_map/psum | solution.py:98
  11.6 82.1 %all-gather.3.cloned.1.call-start = ((), (), s32[]{:S(2)}) async-start(), calls=%async_computation.1 | async-start | bytes 1966080 | tf_op jit(solution)/shard_map/all_gather | solution.py:119
  57.4 73.9 %all-gather.5.cloned.1.call-start = ((), (), s32[]{:S(2)}) async-start(), calls=%async_computation.2 | async-start | bytes 1966080 | tf_op jit(solution)/shard_map/all_gather | solution.py:120
  137.1 3.5 %copy-start.1 = (f32[2,4,256,128]{3,2,1,0:T(8,128)S(1)}, f32[2,4,256,128]{3,2,1,0:T(8,128)}, u32[]{:S(2)}) copy-start(f32[2,4,256,128]{3,2,1,0:T(8,128)} %get-tuple-element.124) | copy-start | bytes 3145732 | tf_op jit(solution)/shard_map/while/body/eval_jaxpr/cond
  144.6 1.0 copy-start.2
  147.7 3.5 %copy-start.1 = (f32[2,4,256,128]{3,2,1,0:T(8,128)S(1)}, f32[2,4,256,128]{3,2,1,0:T(8,128)}, u32[]{:S(2)}) copy-start(f32[2,4,256,128]{3,2,1,0:T(8,128)} %get-tuple-element.124) | copy-start | bytes 3145732 | tf_op jit(solution)/shard_map/while/body/eval_jaxpr/cond
  155.2 1.0 copy-start.2
  158.3 3.5 %copy-start.1 = (f32[2,4,256,128]{3,2,1,0:T(8,128)S(1)}, f32[2,4,256,128]{3,2,1,0:T(8,128)}, u32[]{:S(2)}) copy-start(f32[2,4,256,128]{3,2,1,0:T(8,128)} %get-tuple-element.124) | copy-start | bytes 3145732 | tf_op jit(solution)/shard_map/while/body/eval_jaxpr/cond
  165.8 1.0 copy-start.2
Sparse Core Ops, SparseCore 0:
  11.8 34.2 all-reduce.1
  57.5 36.1 all-gather.2
  95.3 35.8 all-gather.4
